TPU v7x, 512 devices: a whole 4x8x8 slice. The times are simulated.
512 devices in a mesh: rows: 128 (over y, z, core), rep: 4 (over x).
Axes of the slice: x: 4, y: 8, z: 8, core: 2. Of those that a mesh axis runs over, the one named last changes fastest.
Arguments:
- pivots: int32 [2, 256], replicated, may hold values from 0 to 61439, as said below
- previous: float32 [61440, 1536], P('rows', 'rep'), may hold values from -0.3 to 0.3
- columns: float32 [61440, 512], P(('rows', 'rep')), may hold values from -16 to 16
- diagonal: float32 [61440], P(('rows', 'rep')), may hold values from 2 to 6
Outputs:
- vectors: float32 [61440, 512], P(('rows', 'rep'))
- diag_out: float32 [61440], P(('rows', 'rep'))
Inputs may be any that keep to these rules, and one draw needn't show every extreme that they name: 512 different AO-pair indices; the residual blocks at each panel's pivots are positive definite.
All inputs are finite; a program needn't handle non-finite values.
Results may differ from a plain program's by a relative error of at most 0.00011.
Values sent between devices are 32-bit elements; how exact they have to be, the bound alone decides.
A program may use at most 64 MiB of HBM per device.

v0:
```python
import jax
import jax.numpy as jnp
from jax import lax
from jax.sharding import PartitionSpec as P

highest = lax.Precision.HIGHEST


def pick_rows(matrix, local_index):
    length = matrix.shape[0]
    inside = (local_index >= 0) & (local_index < length)
    taken = jnp.take(matrix, jnp.clip(local_index, 0, length - 1), axis=0)
    return jnp.where(inside[:, None], taken, jnp.zeros_like(taken))


def times_transposed(left, right):
    return lax.dot_general(
        left, right, (((1,), (1,)), ((), ())), precision=highest, preferred_element_type=jnp.float32
    )


def solve_right(factor, matrix):
    return jax.scipy.linalg.solve_triangular(factor, matrix.T, lower=True).T


def per_device(pivots, previous, columns, diagonal):
    block_rows = previous.shape[0]
    own_count = columns.shape[0]
    panel_width = columns.shape[1] // 2
    replicas = lax.axis_size("rep")
    row_block = lax.axis_index("rows")
    rep_block = lax.axis_index("rep")
    all_pivots = pivots.reshape(-1)
    picked = pick_rows(previous, all_pivots - row_block * block_rows)
    chosen = lax.psum(picked, "rows")
    resid = columns + lax.psum_scatter(
        -times_transposed(previous, chosen), "rep", scatter_dimension=0, tiled=True
    )
    own_start = (row_block * replicas + rep_block) * own_count
    local_index = all_pivots - own_start
    first_part = resid[:, :panel_width]
    block_one = lax.psum(pick_rows(first_part, local_index[:panel_width]), ("rows", "rep"))
    factor_one = jnp.linalg.cholesky(block_one)
    vec_one = solve_right(factor_one, first_part)
    second_index = local_index[panel_width:]
    cross_rows, block_two = lax.psum(
        (pick_rows(vec_one, second_index), pick_rows(resid[:, panel_width:], second_index)),
        ("rows", "rep"),
    )
    factor_two = jnp.linalg.cholesky(block_two - times_transposed(cross_rows, cross_rows))
    rest = resid[:, panel_width:] - times_transposed(vec_one, cross_rows)
    vec_two = solve_right(factor_two, rest)
    vectors = jnp.concatenate([vec_one, vec_two], axis=1)
    diag_out = diagonal - jnp.sum(vec_one * vec_one, axis=1) - jnp.sum(vec_two * vec_two, axis=1)
    return (vectors, diag_out)


def solution(mesh):
    placed = (P(), P("rows", "rep"), P(("rows", "rep"), None), P(("rows", "rep")))
    return jax.shard_map(
        per_device,
        mesh=mesh,
        in_specs=placed,
        out_specs=(P(("rows", "rep"), None), P(("rows", "rep"))),
        check_vma=False,
    )
```

profile of v0, /device:TPU:1, one launch (start us, length us, event | category | flops | bytes accessed | tf_op | source)
XLA Modules:
  0.0 923.9 jit_solution(11820566420991848047)
XLA Ops:
  7.2 0.0 all-reduce.6.cloned.1.call-start
  7.2 0.7 copy-done.5
  8.1 0.2 copy-done
  8.3 1.6 gather_fusion
  9.9 1.1 select_select_fusion
  11.0 0.0 all-reduce.6.cloned.1.call-update
  11.0 0.0 reduce-scatter.2.cloned.1.call-start
  11.1 201.1 %all-reduce.6.cloned.1.call-done = f32[512,384]{1,0:T(8,128)} async-done(((f32[512,384]{1,0:T(8,128)}), f32[512,384]{1,0:T(8,128)}) %all-reduce.6.cloned.1.call-update) | async-done | bytes 786448 | tf_op jit(solution)/shard_map/psum | solution.py:35
  212.1 3.8 fusion
  216.0 0.0 reduce-scatter.2.cloned.1.call-update
  216.0 0.0 all-reduce.8.cloned.1.call-start
  216.2 25.4 %reduce-scatter.2.cloned.1.call-done = f32[120,512]{1,0:T(8,128)} async-done(((f32[480,512]{1,0:T(8,128)}), f32[120,512]{1,0:T(8,128)}) %reduce-scatter.2.cloned.1.call-update) | async-done | bytes 245776 | tf_op jit(solution)/shard_map/reduce_scatter | solution.py:36
  241.5 1.0 add.60
  242.5 1.0 gather_fusion.1
  243.5 0.1 copy.6
  243.6 0.7 select_select_fusion.5
  244.4 0.2 all-reduce.10.cloned.1.call-start
  244.6 1.0 gather_fusion.2
  245.6 0.1 copy.8
  245.8 273.3 %all-reduce.8.cloned.1.call-done = f32[256,256]{0,1:T(8,128)} async-done(((f32[256,256]{0,1:T(8,128)}), f32[256,256]{0,1:T(8,128)}) %all-reduce.8.cloned.1.call-update) | async-done | bytes 262160 | tf_op jit(solution)/shard_map/psum | solution.py:42
  519.0 1.1 copy.7
  520.3 11.7 %cholesky.130 = f32[128,128]{1,0:T(8,128)S(1)} custom-call(f32[128,128]{1,0:T(8,128)S(1)} %cholesky.194), custom_call_target="Cholesky" | custom-call | tf_op jit(solution)/shard_map/jit(cholesky)/cholesky | solution.py:43
  532.0 9.8 %custom-call.13 = f32[1,128,128]{1,2,0:T(8,128)S(1)} custom-call(f32[1,128,128]{2,1,0:T(8,128)S(1)} %get-tuple-element.55), custom_call_target="InvertDiagBlocksLowerTriangular" | custom-call | tf_op jit(solution)/shard_map/jit(cholesky)/cholesky | solution.py:43
  541.9 0.2 constant_dynamic-update-slice_fusion.3
  542.1 0.3 convolution_subtract_fusion.3
  542.3 11.7 %cholesky.147 = f32[128,128]{1,0:T(8,128)S(1)} custom-call(f32[128,128]{1,0:T(8,128)S(1)} %convolution_subtract_fusion.3), custom_call_target="Cholesky" | custom-call | tf_op jit(solution)/shard_map/jit(cholesky)/cholesky | solution.py:43
  554.1 0.7 compare_reduce_fusion.2
  556.1 0.1 triangular_solve.75
  556.2 4.1 while.4
  556.2 0.7 fusion.37
  556.9 1.3 bitcast_dynamic-update-slice_fusion.4
  558.2 0.7 fusion.37
  558.9 1.3 bitcast_dynamic-update-slice_fusion.4
  560.3 19.9 %custom-call.14 = f32[2,128,128]{1,2,0:T(8,128)S(1)} custom-call(f32[2,128,128]{2,1,0:T(8,128)S(1)} %get-tuple-element.19), custom_call_target="InvertDiagBlocksLowerTriangular" | custom-call | tf_op jit(solution)/shard_map/jit(_solve_triangular)/triangular_solve | solution.py:23
  580.2 0.3 fusion.12
  580.4 0.3 convolution_subtract_fusion.5
  580.7 0.3 fusion.11
  581.0 1.0 gather_fusion.3
  582.0 0.1 copy.9
  582.1 0.9 select_select_fusion.3
  583.0 0.1 multiply_reduce_fusion.1
  583.1 269.4 %all-reduce.10.cloned.1.call-done = (f32[256,256]{0,1:T(8,128)}, f32[256,256]{0,1:T(8,128)}) async-done(((f32[256,256]{0,1:T(8,128)}, f32[256,256]{0,1:T(8,128)}), (f32[256,256]{0,1:T(8,128)}, f32[256,256]{0,1:T(8,128)})) %all-reduce.10.cloned.1.call-update) | async-done | bytes 524304 | tf_op jit(solution)/shard_map/psum | solution.py:46
  852.5 1.3 fusion.1
  853.9 0.6 convolution_subtract_fusion
  854.5 0.1 copy.11
  854.7 11.7 %cholesky.164 = f32[128,128]{1,0:T(8,128)S(1)} custom-call(f32[128,128]{1,0:T(8,128)S(1)} %cholesky.197), custom_call_target="Cholesky" | custom-call | tf_op jit(solution)/shard_map/jit(cholesky)/cholesky | solution.py:50
  866.4 9.8 %custom-call.15 = f32[1,128,128]{1,2,0:T(8,128)S(1)} custom-call(f32[1,128,128]{2,1,0:T(8,128)S(1)} %get-tuple-element.51), custom_call_target="InvertDiagBlocksLowerTriangular" | custom-call | tf_op jit(solution)/shard_map/jit(cholesky)/cholesky | solution.py:50
  876.2 0.2 constant_dynamic-update-slice_fusion.1
  876.5 0.3 convolution_subtract_fusion.2
  876.7 11.9 %cholesky.181 = f32[128,128]{1,0:T(8,128)S(1)} custom-call(f32[128,128]{1,0:T(8,128)S(1)} %convolution_subtract_fusion.2), custom_call_target="Cholesky" | custom-call | tf_op jit(solution)/shard_map/jit(cholesky)/cholesky | solution.py:50
  888.7 0.7 compare_reduce_fusion
  889.4 0.6 compare_reduce_fusion.1
  891.4 4.1 while.5
  891.4 0.6 fusion.38
  892.0 1.4 bitcast_dynamic-update-slice_fusion.5
  893.5 0.6 fusion.38
  894.1 1.4 bitcast_dynamic-update-slice_fusion.5
  895.5 19.7 %custom-call.16 = f32[2,128,128]{1,2,0:T(8,128)S(1)} custom-call(f32[2,128,128]{2,1,0:T(8,128)S(1)} %get-tuple-element.20), custom_call_target="InvertDiagBlocksLowerTriangular" | custom-call | tf_op jit(solution)/shard_map/jit(_solve_triangular)/triangular_solve | solution.py:23
  915.2 0.3 fusion.7
  915.5 0.3 convolution_subtract_fusion.4
  915.8 0.3 fusion.6
  916.0 0.1 multiply_reduce_fusion
  916.2 0.7 pad_maximum_fusion
  916.9 0.5 subtract_subtract_fusion
  (52 shorter events, 0.6 us)
Async XLA Ops:
  7.2 1.1 copy-start
  7.2 204.9 %all-reduce.6.cloned.1.call-start = ((), (), s32[]{:S(2)}) async-start(), calls=%async_computation.1 | async-start | bytes 1572864 | tf_op jit(solution)/shard_map/psum | solution.py:35
  7.2 0.7 copy-start.5
  11.0 230.5 %reduce-scatter.2.cloned.1.call-start = ((), (), s32[]{:S(2)}) async-start(), calls=%async_computation.2 | async-start | bytes 1228800 | tf_op jit(solution)/shard_map/reduce_scatter | solution.py:36
  216.0 25.5 %copy-start.4 = (f32[120,512]{1,0:T(8,128)S(1)}, f32[120,512]{1,0:T(8,128)}, u32[]{:S(2)}) copy-start(f32[120,512]{1,0:T(8,128)} %param.11) | copy-start | bytes 737284
  216.0 303.0 %all-reduce.8.cloned.1.call-start = ((), (), s32[]{:S(2)}) async-start(), calls=%async_computation.3 | async-start | bytes 524288 | tf_op jit(solution)/shard_map/psum | solution.py:42
  244.4 608.1 %all-reduce.10.cloned.1.call-start = ((), (), s32[]{:S(2)}) async-start(), calls=%async_computation.4 | async-start | bytes 1048576 | tf_op jit(solution)/shard_map/psum | solution.py:46
  519.0 1.2 copy-start.2
  852.5 1.3 copy-start.1
  852.5 1.3 copy-start.3
  916.1 0.7 copy-start.6
Sparse Core Ops, SparseCore 0:
  11.2 200.8 all-reduce.5
  216.1 25.3 reduce-scatter.1
  246.5 272.4 all-reduce.7
  583.1 269.3 all-reduce.9
where the time goes:
time: 924 us
  waiting for transfers between devices  769 us (83%)
  other arithmetic  114 us (12%)
  between operations  16.8 us (2%)
  local copies, waits for them, and re-layouts  15.4 us (2%)
    psum x1, waiting for transfers between devices, per_device(): lax.psum(pick_rows(first_part, local_index[:panel_width]), ('rows', 'rep'))  273 us
    psum x1, waiting for transfers between devices, per_device(): lax.psum((pick_rows(vec_one, second_index), pick_rows(resid[:, panel_widt...  269 us
    psum x1, waiting for transfers between devices, per_device(): chosen = lax.psum(picked, 'rows')  201 us
    another operation x5, other arithmetic, solve_right(): return jax.scipy.linalg.solve_triangular(factor, matrix.T, lower=True).T  39.6 us
    another operation x7, other arithmetic, per_device(): jnp.linalg.cholesky(block_two - times_transposed(cross_rows, cross_rows))  34.8 us
    another operation x6, other arithmetic, per_device(): factor_one = jnp.linalg.cholesky(block_one)  34 us
    reduce_scatter x1, waiting for transfers between devices, per_device(): lax.psum_scatter(-times_transposed(previous, chosen), 'rep', scatter_dime...  25.4 us
  transfers between devices with their start and end apart: 4, of which 4 were waited for; matrix products, arithmetic and copies ran while one was open for 0% of the time, Pallas kernels for 0%

commit v1 on v0

v1 whole, which is shorter than its diff:
```python
import functools

import jax
import jax.numpy as jnp
from jax import lax
from jax.experimental import pallas as pl
from jax.experimental.pallas import tpu as pltpu
from jax.sharding import PartitionSpec as P

HIGHEST = lax.Precision.HIGHEST
MESH = pl.DeviceIdType.MESH
PANEL = 256
EARLY = 384
SIDE = 8
REPS = 4
CHUNK = PANEL // 2 // SIDE
WIDTHS = (EARLY + PANEL, EARLY + 2 * PANEL)


def dot_nt(left, right, precision=HIGHEST):
    return lax.dot_general(
        left, right, (((1,), (1,)), ((), ())), precision=precision, preferred_element_type=jnp.float32
    )


def pick(mask, values):
    total = None
    for _ in range(3):
        part = values.astype(jnp.bfloat16)
        values = values - part.astype(jnp.float32)
        term = lax.dot_general(
            mask, part, (((0,), (0,)), ((), ())), preferred_element_type=jnp.float32
        )
        total = term if total is None else total + term
    return total


def kernel(
    pivots_ref, previous_ref, columns_ref,
    g11_ref, g21_ref, g22_ref, resid_ref,
    pick0, pick1, pair0, pair1, half0, half1, first0, first1, own0, own1, second0, second1,
    full0, full1, gpart0, gpart1, gx0, gx1, gsum0, gsum1, partial, rres,
    pair_sems, axis_sems, fwd_sems, gx_sems, gpair_sems, res_sems,
):
    rows = lax.axis_index("rows")
    rep = lax.axis_index("rep")
    core = lax.rem(rows, 2)
    chip_z = lax.rem(rows // 2, SIDE)
    chip_y = rows // (2 * SIDE)
    spot = (1 - core) * chip_y + core * chip_z

    def at(y, z, c):
        return (y * SIDE + z) * 2 + c

    def first_peer(d):
        y = lax.rem(chip_y + (1 - core) * d, SIDE)
        z = lax.rem(chip_z + core * d, SIDE)
        return at(y, z, core), lax.rem(spot + d, SIDE)

    def second_peer(d):
        y = lax.rem(chip_y + core * d, SIDE)
        z = lax.rem(chip_z + (1 - core) * d, SIDE)
        return at(y, z, core)

    partner = at(chip_y, chip_z, 1 - core)
    barrier = pltpu.get_barrier_semaphore()
    for d in range(1, SIDE):
        pl.semaphore_signal(barrier, inc=1, device_id=(first_peer(d)[0], rep), device_id_type=MESH)
        pl.semaphore_signal(barrier, inc=1, device_id=(second_peer(d), rep), device_id_type=MESH)
    for d in range(1, REPS):
        pl.semaphore_signal(barrier, inc=1, device_id=(rows, lax.rem(rep + d, REPS)), device_id_type=MESH)
    pl.semaphore_signal(barrier, inc=1, device_id=(partner, rep), device_id_type=MESH)

    def send(src, dst, sems, slot, where):
        copy = pltpu.make_async_remote_copy(
            src_ref=src, dst_ref=dst, send_sem=sems.at[(0,) + slot], recv_sem=sems.at[(1,) + slot],
            device_id=where, device_id_type=MESH,
        )
        copy.start()
        return copy

    block_rows = previous_ref.shape[0]
    own_rows = columns_ref.shape[0]
    picks, pairs, halves, firsts = (pick0, pick1), (pair0, pair1), (half0, half1), (first0, first1)
    owns, seconds, fulls = (own0, own1), (second0, second1), (full0, full1)
    gparts, gxs, gsums = (gpart0, gpart1), (gx0, gx1), (gsum0, gsum1)

    def make_picks(p):
        index = pivots_ref[p:p + 1, :]
        block = lax.broadcasted_iota(jnp.int32, (block_rows, PANEL), 0) + rows * block_rows
        mask = jnp.where(block == index, 1.0, 0.0).astype(jnp.bfloat16)
        picks[p][:, :EARLY] = pick(mask, previous_ref[...])
        own = lax.broadcasted_iota(jnp.int32, (own_rows, PANEL), 0) + (rows * REPS + rep) * own_rows
        mask = jnp.where(own == index, 1.0, 0.0)
        values = columns_ref[:, :WIDTHS[p] - EARLY]
        pad = jnp.zeros((-own_rows % 16, PANEL), jnp.float32)
        mask = jnp.concatenate([mask, pad], axis=0).astype(jnp.bfloat16)
        pad = jnp.zeros((-own_rows % 16, values.shape[1]), jnp.float32)
        picks[p][:, EARLY:] = pick(mask, jnp.concatenate([values, pad], axis=0))

    def start_pair(p):
        src = picks[p].at[pl.ds((1 - core) * (PANEL // 2), PANEL // 2), :]
        return send(src, pairs[p], pair_sems, (p,), (partner, rep))

    def start_first(p, pair_copy):
        pair_copy.wait()
        halves[p][...] = picks[p][pl.ds(core * (PANEL // 2), PANEL // 2), :] + pairs[p][...]
        copies = []
        for d in (4, 3, 5, 2, 6, 1, 7):
            peer, place = first_peer(d)
            src = halves[p].at[pl.ds(place * CHUNK, CHUNK), :]
            copies.append(send(src, firsts[p].at[d - 1], axis_sems, (p, 0, d - 1), (peer, rep)))
        return copies

    def start_second(p, copies):
        total = halves[p][pl.ds(spot * CHUNK, CHUNK), :]
        for copy in copies:
            copy.wait()
        for d in range(1, SIDE):
            total = total + firsts[p][d - 1]
        owns[p][0] = total
        result = []
        for d in (4, 3, 5, 2, 6, 1, 7):
            result.append(send(owns[p].at[0], seconds[p].at[d - 1], axis_sems, (p, 1, d - 1), (second_peer(d), rep)))
        return result

    def start_gather(p, copies):
        for copy in copies:
            copy.wait()
        total = owns[p][0]
        for d in range(1, SIDE):
            total = total + seconds[p][d - 1]
        owns[p][1] = total
        place = pl.ds(core * (PANEL // 2) + spot * CHUNK, CHUNK)
        fulls[p][place, :] = total
        result = []
        for d in (4, 3, 5, 2, 6, 1, 7):
            peer, _ = first_peer(d)
            result.append(send(owns[p].at[1], fulls[p].at[place, :], axis_sems, (p, 2, d - 1), (peer, rep)))
        result.append(send(owns[p].at[1], fulls[p].at[place, :], fwd_sems, (p, 0), (partner, rep)))
        return result

    def finish_gather(p, copies):
        forwards = []
        order = (4, 3, 5, 2, 6, 1, 7)
        for i in (5, 6, 3, 4, 1, 2, 0):
            d = order[i]
            copies[i].wait()
            source = lax.rem(spot + SIDE - d, SIDE)
            place = pl.ds(core * (PANEL // 2) + source * CHUNK, CHUNK)
            forwards.append(send(fulls[p].at[place, :], fulls[p].at[place, :], fwd_sems, (p, d), (partner, rep)))
        copies[7].wait()
        for copy in forwards:
            copy.wait()

    def start_gsum(p):
        chosen = fulls[p][:, :EARLY]
        cols = fulls[p][:, EARLY:]
        b = PANEL // 2
        if p == 0:
            g = cols - dot_nt(chosen, chosen)
        else:
            g = cols[:, PANEL:] - dot_nt(chosen, chosen)
            g21 = cols[:, :PANEL] - dot_nt(chosen, fulls[0][:, :EARLY])
            gparts[p][3 * b:5 * b] = g21[:, :b]
            gparts[p][5 * b:7 * b] = g21[:, b:]
        gparts[p][0:b] = g[:b, :b]
        gparts[p][b:2 * b] = 0.5 * (g[b:, :b] + g[:b, b:].T)
        gparts[p][2 * b:3 * b] = g[b:, b:]
        size = gparts[p].shape[0] // 2
        mine = pl.ds(core * size, size)
        copies = []
        for d in (2, 1, 3):
            where = (rows, lax.rem(rep + d, REPS))
            copies.append(send(gparts[p].at[mine, :], gxs[p].at[d - 1], gx_sems, (p, d - 1), where))
        return copies

    def start_gpair(p, copies):
        size = gparts[p].shape[0] // 2
        mine = pl.ds(core * size, size)
        for copy in copies:
            copy.wait()
        gsums[p][mine, :] = gparts[p][mine, :] + gxs[p][0] + gxs[p][1] + gxs[p][2]
        return send(gsums[p].at[mine, :], gsums[p].at[mine, :], gpair_sems, (p,), (partner, rep))

    def symmetric(p):
        b = PANEL // 2
        g = gsums[p]
        one, mid, two = g[0:b], g[b:2 * b], g[2 * b:3 * b]
        return 0.5 * (one + one.T), mid, 0.5 * (two + two.T)

    def store_square(ref, parts):
        b = PANEL // 2
        one, mid, two = parts
        ref[:b, :b] = one
        ref[b:, :b] = mid
        ref[:b, b:] = mid.T
        ref[b:, b:] = two

    def start_resid():
        for p in range(2):
            partial[:, p * PANEL:(p + 1) * PANEL] = dot_nt(previous_ref[...], fulls[p][:, :EARLY])
        copies = []
        for d in (2, 1, 3):
            other = lax.rem(rep + d, REPS)
            src = partial.at[pl.ds(other * own_rows, own_rows), :]
            copies.append(send(src, rres.at[d - 1], res_sems, (d - 1,), (rows, other)))
        return copies

    def finish_resid(copies):
        for copy in copies:
            copy.wait()
        mine = partial[pl.ds(rep * own_rows, own_rows), :]
        resid_ref[...] = columns_ref[...] - (((mine + rres[0]) + rres[1]) + rres[2])

    make_picks(0)
    pl.semaphore_wait(barrier, 2 * (SIDE - 1) + REPS)
    pair_a = start_pair(0)
    make_picks(1)
    first_a = start_first(0, pair_a)
    pair_b = start_pair(1)
    second_a = start_second(0, first_a)
    first_b = start_first(1, pair_b)
    gather_a = start_gather(0, second_a)
    second_b = start_second(1, first_b)
    finish_gather(0, gather_a)
    gx_a = start_gsum(0)
    gather_b = start_gather(1, second_b)
    gpair_a = start_gpair(0, gx_a)
    finish_gather(1, gather_b)
    gx_b = start_gsum(1)
    res = start_resid()
    gpair_a.wait()
    store_square(g11_ref, symmetric(0))
    gpair_b = start_gpair(1, gx_b)
    gpair_b.wait()
    b = PANEL // 2
    store_square(g22_ref, symmetric(1))
    g21_ref[:, :b] = gsum1[3 * b:5 * b]
    g21_ref[:, b:] = gsum1[5 * b:7 * b]
    finish_resid(res)


def solve_right(factor, matrix):
    return jax.scipy.linalg.solve_triangular(factor, matrix.T, lower=True).T


def communicate(pivots, previous, columns):
    f32 = jnp.float32
    own_rows = columns.shape[0]
    vmem = lambda *shape: pltpu.VMEM(shape, f32)
    two = lambda build: [build(WIDTHS[0]), build(WIDTHS[1])]
    scratch = []
    scratch += two(lambda w: vmem(PANEL, w))
    scratch += two(lambda w: vmem(PANEL // 2, w))
    scratch += two(lambda w: vmem(PANEL // 2, w))
    scratch += two(lambda w: vmem(SIDE - 1, CHUNK, w))
    scratch += two(lambda w: vmem(2, CHUNK, w))
    scratch += two(lambda w: vmem(SIDE - 1, CHUNK, w))
    scratch += two(lambda w: vmem(PANEL, w))
    scratch += [vmem(384, 128), vmem(896, 128)]
    scratch += [vmem(REPS - 1, 192, 128), vmem(REPS - 1, 448, 128)]
    scratch += [vmem(384, 128), vmem(896, 128)]
    scratch += [vmem(previous.shape[0], 2 * PANEL), vmem(REPS - 1, own_rows, 2 * PANEL)]
    dma = pltpu.SemaphoreType.DMA
    scratch += [
        dma((2, 2)), dma((2, 2, 3, SIDE - 1)), dma((2, 2, SIDE)),
        dma((2, 2, REPS - 1)), dma((2, 2)), dma((2, REPS - 1)),
    ]
    square = jax.ShapeDtypeStruct((PANEL, PANEL), f32)
    return pl.pallas_call(
        kernel,
        out_shape=(square, square, square, jax.ShapeDtypeStruct(columns.shape, f32)),
        in_specs=[pl.BlockSpec(memory_space=pltpu.VMEM)] * 3,
        out_specs=[pl.BlockSpec(memory_space=pltpu.VMEM)] * 4,
        scratch_shapes=scratch,
        compiler_params=pltpu.CompilerParams(collective_id=0, has_side_effects=True),
    )(pivots, previous, columns)


def per_device(pivots, previous, columns, diagonal):
    g11, g21, g22, resid = communicate(pivots, previous, columns)
    first_part, second_part = resid[:, :PANEL], resid[:, PANEL:]
    factor_one = jnp.linalg.cholesky(g11)
    solved = solve_right(factor_one, jnp.concatenate([first_part, g21], axis=0))
    vec_one, cross_rows = solved[:first_part.shape[0]], solved[first_part.shape[0]:]
    factor_two = jnp.linalg.cholesky(g22 - dot_nt(cross_rows, cross_rows))
    rest = second_part - dot_nt(vec_one, cross_rows)
    vec_two = solve_right(factor_two, rest)
    vectors = jnp.concatenate([vec_one, vec_two], axis=1)
    diag_out = diagonal - jnp.sum(vec_one * vec_one, axis=1) - jnp.sum(vec_two * vec_two, axis=1)
    return (vectors, diag_out)


def solution(mesh):
    placed = (P(), P("rows", "rep"), P(("rows", "rep"), None), P(("rows", "rep")))
    return jax.shard_map(
        per_device,
        mesh=mesh,
        in_specs=placed,
        out_specs=(P(("rows", "rep"), None), P(("rows", "rep"))),
        check_vma=False,
    )
```

time: 924 us -> 213 us (0.23)
  waiting for transfers between devices: 769 us -> 0 us
  Pallas kernels: 0 us -> 83.4 us
  between operations: 16.8 us -> 3.6 us
    psum x3 -> x0, waiting for transfers between devices: 744 us -> none  [the longest x1 273 us: per_device(): lax.psum(pick_rows(first_part, local_index[:panel_width]), ('rows', 'rep'))]
    pallas_call x0 -> x1, Pallas kernels: none -> 83.4 us  [communicate(): pl.pallas_call(kernel, out_shape=(square, square, square, jax.ShapeDtypeS...]
    reduce_scatter x1 -> x0, waiting for transfers between devices: 25.4 us -> none  [per_device(): lax.psum_scatter(-times_transposed(previous, chosen), 'rep', scatter_dime...]
  transfers between devices with their start and end apart: 4 -> 0, of which waited for: 4 -> 0; matrix products, arithmetic and copies ran while one was open for 0% -> 0% of each run, Pallas kernels for 0% -> 0%
where the time goes in v1:
time: 213 us; the launch traced here: 212 us
  other arithmetic  110 us (52%)
  Pallas kernels  83.4 us (39%)
  local copies, waits for them, and re-layouts  11.2 us (5%)
  matrix products  3.92 us (2%)
  between operations  3.6 us (2%)
    pallas_call x1, Pallas kernels, communicate(): pl.pallas_call(kernel, out_shape=(square, square, square, jax.ShapeDtypeS...  83.4 us
    another operation x5, other arithmetic, solve_right(): return jax.scipy.linalg.solve_triangular(factor, matrix.T, lower=True).T  39.6 us
    another operation x7, other arithmetic, per_device(): factor_two = jnp.linalg.cholesky(g22 - dot_nt(cross_rows, cross_rows))  34.9 us
    another operation x6, other arithmetic, per_device(): factor_one = jnp.linalg.cholesky(g11)  34.1 us
    another operation x12, local copies, waits for them, and re-layouts  8.1 us

profile of v1, /device:TPU:1, one launch (start us, length us, event | category | flops | bytes accessed | tf_op | source)
XLA Modules:
  0.0 212.5 jit_solution(15680734599427710665)
XLA Ops:
  0.6 83.4 %shard_map.59 = (f32[256,256]{1,0:T(8,128)}, f32[256,256]{1,0:T(8,128)}, f32[256,256]{1,0:T(8,128)}, f32[120,512]{1,0:T(8,128)}) custom-call(s32[2,256]{1,0:T(2,128)} %pivots_ref.1, f32[480,384]{1,0:T(8,128)} %previous_ref.1, f32[120,512]{1,0:T(8,128)} %columns_ref.1), custom_call_target="tpu_custom_call" | custom-call | tf_op jit(solution)/shard_map/pallas_call | solution.py:271
  84.1 0.0 copy-start
  84.1 1.1 copy.6
  85.2 0.0 copy-done
  85.3 11.7 %cholesky.130 = f32[128,128]{1,0:T(8,128)S(1)} custom-call(f32[128,128]{1,0:T(8,128)S(1)} %cholesky.194), custom_call_target="Cholesky" | custom-call | tf_op jit(solution)/shard_map/jit(cholesky)/cholesky | solution.py:284
  97.1 10.0 %custom-call.19 = f32[1,128,128]{1,2,0:T(8,128)S(1)} custom-call(f32[1,128,128]{2,1,0:T(8,128)S(1)} %get-tuple-element.56), custom_call_target="InvertDiagBlocksLowerTriangular" | custom-call | tf_op jit(solution)/shard_map/jit(cholesky)/cholesky | solution.py:284
  107.0 0.2 constant_dynamic-update-slice_fusion.3
  107.3 0.3 convolution_subtract_fusion.4
  107.5 11.7 %cholesky.147 = f32[128,128]{1,0:T(8,128)S(1)} custom-call(f32[128,128]{1,0:T(8,128)S(1)} %convolution_subtract_fusion.4), custom_call_target="Cholesky" | custom-call | tf_op jit(solution)/shard_map/jit(cholesky)/cholesky | solution.py:284
  119.3 0.6 compare_reduce_fusion.2
  121.3 0.1 triangular_solve.96
  121.3 0.0 copy-start.3
  121.4 0.0 copy-start.1
  121.4 4.1 %while.2 = (s32[]{:T(128)}, f32[256,256]{1,0:T(8,128)S(1)}, s32[2,2]{1,0:T(2,128)S(1)}, f32[2,128,128]{2,1,0:T(8,128)S(1)}, s32[]{:T(128)}) while((s32[]{:T(128)}, f32[256,256]{1,0:T(8,128)S(1)}, s32[2,2]{1,0:T(2,128)S(1)}, f32[2,128,128]{2,1,0:T(8,128)S(1)}, s32[]{:T(128)}) %tuple.46), condition=%wide.while_cond, body=%wide.while_body.sunk | while | flops 2 | bytes 131181 | solution.py:245
  121.4 0.7 fusion.32
  122.1 1.3 bitcast_dynamic-update-slice_fusion.4
  123.4 0.7 fusion.32
  124.1 1.3 bitcast_dynamic-update-slice_fusion.4
  125.5 19.9 %custom-call.16 = f32[2,128,128]{1,2,0:T(8,128)S(1)} custom-call(f32[2,128,128]{2,1,0:T(8,128)S(1)} %get-tuple-element.18), custom_call_target="InvertDiagBlocksLowerTriangular" | custom-call | tf_op jit(solution)/shard_map/jit(_solve_triangular)/triangular_solve | solution.py:245
  145.4 0.0 copy-done.3
  145.4 0.0 copy-done.1
  145.4 0.5 fusion.5
  145.9 0.5 convolution_subtract_fusion.1
  146.4 0.5 fusion.13
  146.9 0.0 copy-start.2
  146.9 0.9 copy-done.2
  147.8 0.1 copy.7
  147.9 0.4 convolution_subtract_fusion
  148.4 0.1 copy.9
  148.6 11.7 %cholesky.164 = f32[128,128]{1,0:T(8,128)S(1)} custom-call(f32[128,128]{1,0:T(8,128)S(1)} %cholesky.197), custom_call_target="Cholesky" | custom-call | tf_op jit(solution)/shard_map/jit(cholesky)/cholesky | solution.py:287
  160.3 9.8 %custom-call.20 = f32[1,128,128]{1,2,0:T(8,128)S(1)} custom-call(f32[1,128,128]{2,1,0:T(8,128)S(1)} %get-tuple-element.52), custom_call_target="InvertDiagBlocksLowerTriangular" | custom-call | tf_op jit(solution)/shard_map/jit(cholesky)/cholesky | solution.py:287
  170.1 0.2 constant_dynamic-update-slice_fusion.1
  170.4 0.3 convolution_subtract_fusion.3
  170.6 11.9 %cholesky.181 = f32[128,128]{1,0:T(8,128)S(1)} custom-call(f32[128,128]{1,0:T(8,128)S(1)} %convolution_subtract_fusion.3), custom_call_target="Cholesky" | custom-call | tf_op jit(solution)/shard_map/jit(cholesky)/cholesky | solution.py:287
  182.6 0.7 compare_reduce_fusion
  183.3 0.6 compare_reduce_fusion.1
  185.3 4.1 %while.3 = (s32[]{:T(128)}, f32[256,256]{1,0:T(8,128)S(1)}, s32[2,2]{1,0:T(2,128)S(1)}, f32[2,128,128]{2,1,0:T(8,128)S(1)}, s32[]{:T(128)}) while((s32[]{:T(128)}, f32[256,256]{1,0:T(8,128)S(1)}, s32[2,2]{1,0:T(2,128)S(1)}, f32[2,128,128]{2,1,0:T(8,128)S(1)}, s32[]{:T(128)}) %tuple.52), condition=%wide.while_cond.1, body=%wide.while_body.1.sunk | while | flops 2 | bytes 131181 | solution.py:245
  185.3 0.6 fusion.33
  185.9 1.4 bitcast_dynamic-update-slice_fusion.5
  187.4 0.6 fusion.33
  188.0 1.4 bitcast_dynamic-update-slice_fusion.5
  189.4 19.7 %custom-call.17 = f32[2,128,128]{1,2,0:T(8,128)S(1)} custom-call(f32[2,128,128]{2,1,0:T(8,128)S(1)} %get-tuple-element.26), custom_call_target="InvertDiagBlocksLowerTriangular" | custom-call | tf_op jit(solution)/shard_map/jit(_solve_triangular)/triangular_solve | solution.py:245
  209.1 0.4 fusion
  209.5 0.3 fusion.9
  209.8 0.3 convolution_subtract_fusion.5
  210.1 0.3 fusion.8
  210.3 0.1 multiply_reduce_fusion
  210.4 0.1 multiply_reduce_fusion.1
  210.6 0.0 copy-start.4
  210.6 0.7 copy-done.4
  211.2 0.5 subtract_subtract_fusion
  211.7 0.7 pad_maximum_fusion
  (23 shorter events, 0.5 us)
Async XLA Ops:
  84.1 1.2 copy-start
  121.3 24.0 %copy-start.3 = (f32[120,512]{1,0:T(8,128)S(1)}, f32[120,512]{1,0:T(8,128)}, u32[]{:S(2)}) copy-start(f32[120,512]{1,0:T(8,128)} %get-tuple-element.8) | copy-start | bytes 737284
  121.4 24.0 %copy-start.1 = (f32[256,256]{1,0:T(8,128)S(1)}, f32[256,256]{1,0:T(8,128)}, u32[]{:S(2)}) copy-start(f32[256,256]{1,0:T(8,128)} %get-tuple-element.9) | copy-start | bytes 786436
  146.9 1.0 copy-start.2
  210.6 0.7 copy-start.4

commit v2 on v1

--- a/solution.py
+++ b/solution.py
@@ -241,8 +241,100 @@
     finish_resid(res)
 
 
-def solve_right(factor, matrix):
-    return jax.scipy.linalg.solve_triangular(factor, matrix.T, lower=True).T
+BASE = 32
+TILES = BASE // 8
+
+
+def dot_tn(left, right):
+    return lax.dot_general(
+        left, right, (((0,), (0,)), ((), ())), precision=HIGHEST, preferred_element_type=jnp.float32
+    )
+
+
+def spread(tile, row):
+    return jnp.broadcast_to(tile[row:row + 1, :], tile.shape)
+
+
+def eliminate(square, wide):
+    sub = lax.broadcasted_iota(jnp.int32, (8, 128), 0)
+    cols = []
+    for k in range(BASE):
+        cols.append([None] * TILES)
+        for v in range(k // 8, TILES):
+            cols[k][v] = jnp.broadcast_to(square[8 * v:8 * v + 8, k:k + 1], (8, 128))
+    lanes = wide.shape[1] // 128
+    work = [[wide[8 * v:8 * v + 8, 128 * l:128 * l + 128] for l in range(lanes)] for v in range(TILES)]
+    pivots = []
+    for j in range(BASE):
+        top, row = j // 8, j % 8
+        pivot = spread(cols[j][top], row)
+        pivots.append(pivot)
+        inverse = 1.0 / pivot
+        factor = [None] * TILES
+        for v in range(top, TILES):
+            value = cols[j][v] * inverse
+            factor[v] = jnp.where(sub > row, value, 0.0) if v == top else value
+        for k in range(j + 1, BASE):
+            value = spread(cols[j][k // 8], k % 8)
+            for v in range(k // 8, TILES):
+                cols[k][v] = cols[k][v] - factor[v] * value
+        for l in range(lanes):
+            value = spread(work[top][l], row)
+            for v in range(top, TILES):
+                work[v][l] = work[v][l] - factor[v] * value
+    out = []
+    for v in range(TILES):
+        pivot = pivots[8 * v]
+        for s in range(1, 8):
+            pivot = jnp.where(sub == s, pivots[8 * v + s], pivot)
+        scale = lax.rsqrt(pivot)
+        scale = scale * (1.5 - 0.5 * pivot * scale * scale)
+        out.append(jnp.concatenate([work[v][l] * scale for l in range(lanes)], axis=1))
+    return jnp.concatenate(out, axis=0)
+
+
+def factor_inverse(block_ref, upper_ref):
+    for k in range(PANEL // BASE):
+        rows = slice(k * BASE, k * BASE + BASE)
+        lane = lax.broadcasted_iota(jnp.int32, (BASE, PANEL), 1)
+        sub = lax.broadcasted_iota(jnp.int32, (BASE, PANEL), 0)
+        wide = jnp.concatenate([block_ref[rows, :], jnp.where(lane == sub + k * BASE, 1.0, 0.0)], axis=1)
+        for done in (slice(0, (k - 1) * BASE), slice(max(k - 1, 0) * BASE, k * BASE)):
+            if done.stop > done.start:
+                wide = wide - dot_tn(upper_ref[done, rows], upper_ref[done, :])
+        upper_ref[rows, :] = eliminate(wide[:, rows], wide)
+
+
+def factor_kernel(g11_ref, g21_ref, g22_ref, resid_ref, diagonal_ref, vectors_ref, diag_ref, upper, cross, block):
+    factor_inverse(g11_ref, upper)
+    inverse = upper[:, PANEL:]
+    cross[...] = dot_nt(g21_ref[...], inverse)
+    block[...] = g22_ref[...] - dot_nt(cross[...], cross[...])
+    vec_one = dot_nt(resid_ref[:, :PANEL], inverse)
+    vectors_ref[:, :PANEL] = vec_one
+    vectors_ref[:, PANEL:] = resid_ref[:, PANEL:] - dot_nt(vec_one, cross[...])
+    factor_inverse(block, upper)
+    vec_two = dot_nt(vectors_ref[:, PANEL:], upper[:, PANEL:])
+    vectors_ref[:, PANEL:] = vec_two
+    ones = jnp.ones((8, PANEL), jnp.float32)
+    sums = dot_nt(ones, vec_one * vec_one) + dot_nt(ones, vec_two * vec_two)
+    diag_ref[...] = diagonal_ref[...] - sums[0:1, :]
+
+
+def factorise(g11, g21, g22, resid, diagonal):
+    f32 = jnp.float32
+    count = resid.shape[0]
+    vmem = pl.BlockSpec(memory_space=pltpu.VMEM)
+    vectors, diag = pl.pallas_call(
+        factor_kernel,
+        out_shape=(jax.ShapeDtypeStruct(resid.shape, f32), jax.ShapeDtypeStruct((1, count), f32)),
+        in_specs=[vmem] * 5,
+        out_specs=[vmem] * 2,
+        scratch_shapes=[
+            pltpu.VMEM((PANEL, 2 * PANEL), f32), pltpu.VMEM((PANEL, PANEL), f32), pltpu.VMEM((PANEL, PANEL), f32),
+        ],
+    )(g11, g21, g22, resid, diagonal.reshape(1, count))
+    return vectors, diag.reshape(count)
 
 
 def communicate(pivots, previous, columns):
@@ -280,16 +372,7 @@
 
 def per_device(pivots, previous, columns, diagonal):
     g11, g21, g22, resid = communicate(pivots, previous, columns)
-    first_part, second_part = resid[:, :PANEL], resid[:, PANEL:]
-    factor_one = jnp.linalg.cholesky(g11)
-    solved = solve_right(factor_one, jnp.concatenate([first_part, g21], axis=0))
-    vec_one, cross_rows = solved[:first_part.shape[0]], solved[first_part.shape[0]:]
-    factor_two = jnp.linalg.cholesky(g22 - dot_nt(cross_rows, cross_rows))
-    rest = second_part - dot_nt(vec_one, cross_rows)
-    vec_two = solve_right(factor_two, rest)
-    vectors = jnp.concatenate([vec_one, vec_two], axis=1)
-    diag_out = diagonal - jnp.sum(vec_one * vec_one, axis=1) - jnp.sum(vec_two * vec_two, axis=1)
-    return (vectors, diag_out)
+    return factorise(g11, g21, g22, resid, diagonal)
 
 
 def solution(mesh):

time: 213 us -> 104 us (0.49)
  other arithmetic: 110 us -> 0 us
  Pallas kernels: 83.4 us -> 103 us
  local copies, waits for them, and re-layouts: 11.2 us -> 0 us
  matrix products: 3.92 us -> 0 us
  between operations: 3.6 us -> 0.64 us
    another operation x18 -> x0, other arithmetic: 109 us -> none  [the longest x5 39.6 us: solve_right(): return jax.scipy.linalg.solve_triangular(factor, matrix.T, lower=True).T]
    pallas_call x0 -> x1, Pallas kernels: none -> 19.3 us  [factorise(): pl.pallas_call(factor_kernel, out_shape=(jax.ShapeDtypeStruct(resid.shape...]
    another operation x17 -> x0, local copies, waits for them, and re-layouts: 8.22 us -> none
    another operation x10 -> x0, matrix products: 3.11 us -> none  [the longest x6 2.17 us: solve_right(): return jax.scipy.linalg.solve_triangular(factor, matrix.T, lower=True).T]
where the time goes in v2:
time: 104 us; the launch traced here: 103 us
  Pallas kernels  103 us (99%)
    pallas_call x1, Pallas kernels, communicate(): pl.pallas_call(kernel, out_shape=(square, square, square, jax.ShapeDtypeS...  83.5 us
    pallas_call x1, Pallas kernels, factorise(): pl.pallas_call(factor_kernel, out_shape=(jax.ShapeDtypeStruct(resid.shape...  19.3 us

profile of v2, /device:TPU:1, one launch (start us, length us, event | category | flops | bytes accessed | tf_op | source)
XLA Modules:
  0.0 103.3 jit_solution(8942248207814986048)
XLA Ops:
  0.6 83.5 %shard_map.59 = (f32[256,256]{1,0:T(8,128)}, f32[256,256]{1,0:T(8,128)}, f32[256,256]{1,0:T(8,128)}, f32[120,512]{1,0:T(8,128)}) custom-call(s32[2,256]{1,0:T(2,128)} %pivots_ref.1, f32[480,384]{1,0:T(8,128)} %previous_ref.1, f32[120,512]{1,0:T(8,128)} %columns_ref.1), custom_call_target="tpu_custom_call" | custom-call | tf_op jit(solution)/shard_map/pallas_call | solution.py:363
  84.1 19.3 %shard_map.60 = (f32[120,512]{1,0:T(8,128)}, f32[1,120]{1,0:T(1,128)}) custom-call(f32[256,256]{1,0:T(8,128)} %get-tuple-element.8.g11_ref, f32[256,256]{1,0:T(8,128)} %get-tuple-element.9.g21_ref, f32[256,256]{1,0:T(8,128)} %get-tuple-element.10.g22_ref, f32[120,512]{1,0:T(8,128)} %get-tuple-element.11.resid_ref, f32[1,120]{1,0:T(1,128)} %bitcast.2), custom_call_target="tpu_custom_call" | custom-call | tf_op jit(solution)/shard_map/pallas_call | solution.py:328

commit v3 on v0

v3 whole, which is shorter than its diff:
```python
import functools

import jax
import jax.numpy as jnp
from jax import lax
from jax.experimental import pallas as pl
from jax.experimental.pallas import tpu as pltpu
from jax.sharding import PartitionSpec as P

HIGHEST = lax.Precision.HIGHEST
MESH = pl.DeviceIdType.MESH
BLOCK = 128
BLOCKS = 4
HALF = BLOCK // 2
EARLY = 384
SIDE = 8
REPS = 4
CHUNK = HALF // SIDE
WIDTHS = tuple(EARLY + BLOCK * (s + 1) for s in range(BLOCKS))
ORDER = (4, 3, 5, 2, 6, 1, 7)
BASE = 32
TILES = BASE // 8


def dot_tn(left, right):
    return lax.dot_general(
        left, right, (((0,), (0,)), ((), ())), precision=HIGHEST, preferred_element_type=jnp.float32
    )


def spread(tile, row):
    return jnp.broadcast_to(tile[row:row + 1, :], tile.shape)


def eliminate(square, wide):
    sub = lax.broadcasted_iota(jnp.int32, (8, 128), 0)
    cols = []
    for k in range(BASE):
        cols.append([None] * TILES)
        for v in range(k // 8, TILES):
            cols[k][v] = jnp.broadcast_to(square[8 * v:8 * v + 8, k:k + 1], (8, 128))
    lanes = wide.shape[1] // 128
    work = [[wide[8 * v:8 * v + 8, 128 * l:128 * l + 128] for l in range(lanes)] for v in range(TILES)]
    pivots = []
    for j in range(BASE):
        top, row = j // 8, j % 8
        pivot = spread(cols[j][top], row)
        pivots.append(pivot)
        inverse = 1.0 / pivot
        factor = [None] * TILES
        for v in range(top, TILES):
            value = cols[j][v] * inverse
            factor[v] = jnp.where(sub > row, value, 0.0) if v == top else value
        for k in range(j + 1, BASE):
            value = spread(cols[j][k // 8], k % 8)
            for v in range(k // 8, TILES):
                cols[k][v] = cols[k][v] - factor[v] * value
        for l in range(lanes):
            value = spread(work[top][l], row)
            for v in range(top, TILES):
                work[v][l] = work[v][l] - factor[v] * value
    out = []
    for v in range(TILES):
        pivot = pivots[8 * v]
        for s in range(1, 8):
            pivot = jnp.where(sub == s, pivots[8 * v + s], pivot)
        scale = lax.rsqrt(pivot)
        scale = scale * (1.5 - 0.5 * pivot * scale * scale)
        out.append(jnp.concatenate([work[v][l] * scale for l in range(lanes)], axis=1))
    return jnp.concatenate(out, axis=0)


def dot_nt(left, right, precision=HIGHEST):
    return lax.dot_general(
        left, right, (((1,), (1,)), ((), ())), precision=precision, preferred_element_type=jnp.float32
    )


def split(values):
    parts = []
    for _ in range(3):
        part = values.astype(jnp.bfloat16)
        values = values - part.astype(jnp.float32)
        parts.append(part)
    return parts


def pick(mask, parts):
    total = None
    for part in parts:
        term = lax.dot_general(mask, part, (((0,), (0,)), ((), ())), preferred_element_type=jnp.float32)
        total = term if total is None else total + term
    return total


def block_cols(s):
    return slice(s * BLOCK, s * BLOCK + BLOCK)


def kernel(pivots_ref, previous_ref, columns_ref, diagonal_ref, vectors_ref, diag_ref, *scratch):
    picks, pairs, halves, firsts, owns, seconds, fulls, gparts, gxs, gsums, partials, rress = (
        scratch[BLOCKS * n:BLOCKS * n + BLOCKS] for n in range(12)
    )
    prev_parts, col_parts, stash, upper, lower, inverse = scratch[12 * BLOCKS:12 * BLOCKS + 6]
    pair_sems, axis_sems, fwd_sems, gx_sems, gpair_sems, res_sems = scratch[12 * BLOCKS + 6:]
    rows = lax.axis_index("rows")
    rep = lax.axis_index("rep")
    core = lax.rem(rows, 2)
    chip_z = lax.rem(rows // 2, SIDE)
    chip_y = rows // (2 * SIDE)
    spot = (1 - core) * chip_y + core * chip_z
    block_rows = previous_ref.shape[0]
    own_rows = columns_ref.shape[0]

    def at(y, z, c):
        return (y * SIDE + z) * 2 + c

    def first_peer(d):
        y = lax.rem(chip_y + (1 - core) * d, SIDE)
        z = lax.rem(chip_z + core * d, SIDE)
        return at(y, z, core), lax.rem(spot + d, SIDE)

    def second_peer(d):
        y = lax.rem(chip_y + core * d, SIDE)
        z = lax.rem(chip_z + (1 - core) * d, SIDE)
        return at(y, z, core)

    partner = at(chip_y, chip_z, 1 - core)
    barrier = pltpu.get_barrier_semaphore()
    for d in range(1, SIDE):
        pl.semaphore_signal(barrier, inc=1, device_id=(first_peer(d)[0], rep), device_id_type=MESH)
        pl.semaphore_signal(barrier, inc=1, device_id=(second_peer(d), rep), device_id_type=MESH)
    for d in range(1, REPS):
        pl.semaphore_signal(barrier, inc=1, device_id=(rows, lax.rem(rep + d, REPS)), device_id_type=MESH)
    pl.semaphore_signal(barrier, inc=1, device_id=(partner, rep), device_id_type=MESH)

    def send(src, dst, sems, slot, where):
        copy = pltpu.make_async_remote_copy(
            src_ref=src, dst_ref=dst, send_sem=sems.at[(0,) + slot], recv_sem=sems.at[(1,) + slot],
            device_id=where, device_id_type=MESH,
        )
        copy.start()
        return copy

    flying = {}

    def make_parts():
        for n, part in enumerate(split(previous_ref[...])):
            prev_parts[n] = part
        pad = jnp.zeros((BLOCK - own_rows, BLOCKS * BLOCK), jnp.float32)
        for n, part in enumerate(split(jnp.concatenate([columns_ref[...], pad], axis=0))):
            col_parts[n] = part

    def make_picks(s):
        index = pivots_ref[s // 2:s // 2 + 1, block_cols(s % 2)]
        block = lax.broadcasted_iota(jnp.int32, (block_rows, BLOCK), 0) + rows * block_rows
        mask = jnp.where(block == index, 1.0, 0.0).astype(jnp.bfloat16)
        picks[s][:, :EARLY] = pick(mask, [prev_parts[n] for n in range(3)])
        place = lax.broadcasted_iota(jnp.int32, (BLOCK, BLOCK), 0)
        own = place + (rows * REPS + rep) * own_rows
        mask = jnp.where((own == index) & (place < own_rows), 1.0, 0.0).astype(jnp.bfloat16)
        wide = (s + 1 + (s + 1) % 2) * BLOCK
        found = pick(mask, [col_parts[n, :, :wide] for n in range(3)])
        same = found[:, block_cols(s)]
        same = 0.5 * (same + same.T)
        if s % 2 == 0:
            stash[s // 2] = found[:, block_cols(s + 1)]
            if s:
                picks[s][:, EARLY:EARLY + s * BLOCK] = found[:, :s * BLOCK]
        else:
            if s > 1:
                picks[s][:, EARLY:EARLY + (s - 1) * BLOCK] = found[:, :(s - 1) * BLOCK]
            mid = 0.5 * (found[:, block_cols(s - 1)] + stash[s // 2].T)
            picks[s][:, EARLY + (s - 1) * BLOCK:EARLY + s * BLOCK] = mid
        picks[s][:, EARLY + s * BLOCK:] = same

    def pair(s):
        src = picks[s].at[pl.ds((1 - core) * HALF, HALF), :]
        flying["pair", s] = send(src, pairs[s], pair_sems, (s,), (partner, rep))

    def first(s):
        flying["pair", s].wait()
        halves[s][...] = picks[s][pl.ds(core * HALF, HALF), :] + pairs[s][...]
        flying["first", s] = []
        for d in ORDER:
            peer, place = first_peer(d)
            src = halves[s].at[pl.ds(place * CHUNK, CHUNK), :]
            flying["first", s].append(send(src, firsts[s].at[d - 1], axis_sems, (s, 0, d - 1), (peer, rep)))

    def second(s):
        total = halves[s][pl.ds(spot * CHUNK, CHUNK), :]
        for copy in flying["first", s]:
            copy.wait()
        for d in range(1, SIDE):
            total = total + firsts[s][d - 1]
        owns[s][0] = total
        flying["second", s] = []
        for d in ORDER:
            where = (second_peer(d), rep)
            flying["second", s].append(send(owns[s].at[0], seconds[s].at[d - 1], axis_sems, (s, 1, d - 1), where))

    def gather(s):
        for copy in flying["second", s]:
            copy.wait()
        total = owns[s][0]
        for d in range(1, SIDE):
            total = total + seconds[s][d - 1]
        owns[s][1] = total
        place = pl.ds(core * HALF + spot * CHUNK, CHUNK)
        fulls[s][place, :] = total
        flying["gather", s] = {}
        for d in ORDER:
            where = (first_peer(d)[0], rep)
            flying["gather", s][d] = send(owns[s].at[1], fulls[s].at[place, :], axis_sems, (s, 2, d - 1), where)
        flying["gather", s][0] = send(owns[s].at[1], fulls[s].at[place, :], fwd_sems, (s, 0), (partner, rep))

    def forward(s):
        flying["forward", s] = []
        for d in (1, 7, 2, 6, 3, 5, 4):
            flying["gather", s][d].wait()
            source = lax.rem(spot + SIDE - d, SIDE)
            place = pl.ds(core * HALF + source * CHUNK, CHUNK)
            here = fulls[s].at[place, :]
            flying["forward", s].append(send(here, here, fwd_sems, (s, d), (partner, rep)))

    def gsum(s):
        flying["gather", s][0].wait()
        for copy in flying["forward", s]:
            copy.wait()
        chosen = fulls[s][:, :EARLY]
        for t in range(s + 1):
            found = fulls[s][:, EARLY + t * BLOCK:EARLY + t * BLOCK + BLOCK]
            gparts[s][:, block_cols(t)] = found - dot_nt(chosen, fulls[t][:, :EARLY])
        mine = pl.ds(core * HALF, HALF)
        flying["gsum", s] = []
        for d in (2, 1, 3):
            where = (rows, lax.rem(rep + d, REPS))
            flying["gsum", s].append(send(gparts[s].at[mine, :], gxs[s].at[d - 1], gx_sems, (s, d - 1), where))

    def gpair(s):
        mine = pl.ds(core * HALF, HALF)
        for copy in flying["gsum", s]:
            copy.wait()
        gsums[s][mine, :] = gparts[s][mine, :] + gxs[s][0] + gxs[s][1] + gxs[s][2]
        flying["gpair", s] = send(gsums[s].at[mine, :], gsums[s].at[mine, :], gpair_sems, (s,), (partner, rep))

    def scatter(s):
        partials[s][...] = dot_nt(previous_ref[...], fulls[s][:, :EARLY])
        flying["scatter", s] = []
        for d in (2, 1, 3):
            other = lax.rem(rep + d, REPS)
            src = partials[s].at[pl.ds(other * own_rows, own_rows), :]
            flying["scatter", s].append(send(src, rress[s].at[d - 1], res_sems, (s, d - 1), (rows, other)))

    def resid(s):
        for copy in flying["scatter", s]:
            copy.wait()
        mine = partials[s][pl.ds(rep * own_rows, own_rows), :]
        total = columns_ref[:, block_cols(s)] - (((mine + rress[s][0]) + rress[s][1]) + rress[s][2])
        for u in range(s):
            total = total - dot_nt(vectors_ref[:, block_cols(u)], lower[s, :, block_cols(u)])
        vectors_ref[:, block_cols(s)] = total

    def solve(s):
        vectors_ref[:, block_cols(s)] = dot_nt(vectors_ref[:, block_cols(s)], inverse[s])

    def factor(s, gaps):
        flying["gpair", s].wait()
        block = gsums[s][:, block_cols(s)]
        for t in range(s):
            row = gsums[s][:, block_cols(t)]
            for u in range(t):
                row = row - dot_nt(lower[s, :, block_cols(u)], lower[t, :, block_cols(u)])
            row = dot_nt(row, inverse[t])
            lower[s, :, block_cols(t)] = row
            block = block - dot_nt(row, row)
        gparts[s][:, block_cols(s)] = block
        for k in range(BLOCK // BASE):
            here = slice(k * BASE, k * BASE + BASE)
            lane = lax.broadcasted_iota(jnp.int32, (BASE, BLOCK), 1)
            sub = lax.broadcasted_iota(jnp.int32, (BASE, BLOCK), 0)
            eye = jnp.where(lane == sub + k * BASE, 1.0, 0.0)
            wide = jnp.concatenate([gparts[s][here, block_cols(s)], eye], axis=1)
            for done in (slice(0, (k - 1) * BASE), slice(max(k - 1, 0) * BASE, k * BASE)):
                if done.stop > done.start:
                    wide = wide - dot_tn(upper[done, here], upper[done, :])
            upper[here, :] = eliminate(wide[:, here], wide)
            if k == BLOCK // BASE - 1:
                inverse[s] = upper[:, BLOCK:]
            for step in gaps.get(k, ()):
                step()

    def later(work, s):
        return lambda: work(s)

    make_parts()
    make_picks(0)
    pl.semaphore_wait(barrier, 2 * (SIDE - 1) + REPS)
    pair(0)
    make_picks(1)
    first(0)
    pair(1)
    make_picks(2)
    make_picks(3)
    second(0)
    first(1)
    pair(2)
    gather(0)
    second(1)
    forward(0)
    gsum(0)
    gather(1)
    first(2)
    pair(3)
    gpair(0)
    forward(1)
    gsum(1)
    second(2)
    factor(0, {
        0: (later(gpair, 1), later(first, 3)),
        1: (later(gather, 2), later(scatter, 0)),
        2: (later(second, 3), later(forward, 2)),
        3: (later(gsum, 2), later(scatter, 1)),
    })
    factor(1, {
        0: (later(gather, 3), later(resid, 0), later(solve, 0)),
        1: (later(gpair, 2),),
        2: (later(forward, 3), later(resid, 1)),
        3: (later(gsum, 3), later(solve, 1)),
    })
    factor(2, {
        0: (later(scatter, 2),),
        1: (later(gpair, 3),),
        2: (later(scatter, 3),),
        3: (later(resid, 2), later(solve, 2)),
    })
    factor(3, {3: (later(resid, 3), later(solve, 3))})
    ones = jnp.ones((8, BLOCK), jnp.float32)
    sums = diagonal_ref[...]
    for s in range(BLOCKS):
        vec = vectors_ref[:, block_cols(s)]
        sums = sums - dot_nt(ones, vec * vec)[0:1, :]
    diag_ref[...] = sums


def per_device(pivots, previous, columns, diagonal):
    f32 = jnp.float32
    own_rows = columns.shape[0]
    block_rows = previous.shape[0]
    vmem = lambda *shape: pltpu.VMEM(shape, f32)
    each = lambda build: [build(s) for s in range(BLOCKS)]
    scratch = []
    scratch += each(lambda s: vmem(BLOCK, WIDTHS[s]))
    scratch += each(lambda s: vmem(HALF, WIDTHS[s]))
    scratch += each(lambda s: vmem(HALF, WIDTHS[s]))
    scratch += each(lambda s: vmem(SIDE - 1, CHUNK, WIDTHS[s]))
    scratch += each(lambda s: vmem(2, CHUNK, WIDTHS[s]))
    scratch += each(lambda s: vmem(SIDE - 1, CHUNK, WIDTHS[s]))
    scratch += each(lambda s: vmem(BLOCK, WIDTHS[s]))
    scratch += each(lambda s: vmem(BLOCK, BLOCK * (s + 1)))
    scratch += each(lambda s: vmem(REPS - 1, HALF, BLOCK * (s + 1)))
    scratch += each(lambda s: vmem(BLOCK, BLOCK * (s + 1)))
    scratch += each(lambda s: vmem(block_rows, BLOCK))
    scratch += each(lambda s: vmem(REPS - 1, own_rows, BLOCK))
    scratch += [
        pltpu.VMEM((3, block_rows, EARLY), jnp.bfloat16), pltpu.VMEM((3, BLOCK, BLOCKS * BLOCK), jnp.bfloat16),
        vmem(2, BLOCK, BLOCK), vmem(BLOCK, 2 * BLOCK), vmem(BLOCKS, BLOCK, BLOCKS * BLOCK), vmem(BLOCKS, BLOCK, BLOCK),
    ]
    dma = pltpu.SemaphoreType.DMA
    scratch += [
        dma((2, BLOCKS)), dma((2, BLOCKS, 3, SIDE - 1)), dma((2, BLOCKS, SIDE)),
        dma((2, BLOCKS, REPS - 1)), dma((2, BLOCKS)), dma((2, BLOCKS, REPS - 1)),
    ]
    space = pl.BlockSpec(memory_space=pltpu.VMEM)
    vectors, diag = pl.pallas_call(
        kernel,
        out_shape=(jax.ShapeDtypeStruct(columns.shape, f32), jax.ShapeDtypeStruct((1, own_rows), f32)),
        in_specs=[space] * 4,
        out_specs=[space] * 2,
        scratch_shapes=scratch,
        compiler_params=pltpu.CompilerParams(collective_id=0, has_side_effects=True),
    )(pivots, previous, columns, diagonal.reshape(1, own_rows))
    return vectors, diag.reshape(own_rows)


def solution(mesh):
    placed = (P(), P("rows", "rep"), P(("rows", "rep"), None), P(("rows", "rep")))
    return jax.shard_map(
        per_device,
        mesh=mesh,
        in_specs=placed,
        out_specs=(P(("rows", "rep"), None), P(("rows", "rep"))),
        check_vma=False,
    )
```

time: 924 us -> 93 us (0.10)
  waiting for transfers between devices: 769 us -> 0 us
  other arithmetic: 114 us -> 0 us
  Pallas kernels: 0 us -> 90 us
  between operations: 16.8 us -> 0.65 us
  local copies, waits for them, and re-layouts: 15.4 us -> 2.17 us
    psum x3 -> x0, waiting for transfers between devices: 744 us -> none  [the longest x1 273 us: per_device(): lax.psum(pick_rows(first_part, local_index[:panel_width]), ('rows', 'rep'))]
    another operation x18 -> x0, other arithmetic: 109 us -> none  [the longest x5 39.6 us: solve_right(): return jax.scipy.linalg.solve_triangular(factor, matrix.T, lower=True).T]
    pallas_call x0 -> x1, Pallas kernels: none -> 90 us  [per_device(): pl.pallas_call(kernel, out_shape=(jax.ShapeDtypeStruct(columns.shape, f32...]
    reduce_scatter x1 -> x0, waiting for transfers between devices: 25.4 us -> none  [per_device(): lax.psum_scatter(-times_transposed(previous, chosen), 'rep', scatter_dime...]
  transfers between devices with their start and end apart: 4 -> 0, of which waited for: 4 -> 0; matrix products, arithmetic and copies ran while one was open for 0% -> 0% of each run, Pallas kernels for 0% -> 0%
where the time goes in v3:
time: 93 us; the launch traced here: 92.8 us
  Pallas kernels  90 us (97%)
  local copies, waits for them, and re-layouts  2.17 us (2%)
    pallas_call x1, Pallas kernels, per_device(): pl.pallas_call(kernel, out_shape=(jax.ShapeDtypeStruct(columns.shape, f32...  90 us
    unnamed x4, local copies, waits for them, and re-layouts  2.17 us

profile of v3, /device:TPU:1, one launch (start us, length us, event | category | flops | bytes accessed | tf_op | source)
XLA Modules:
  0.0 92.8 jit_solution(11264722244579819222)
XLA Ops:
  0.6 90.0 %shard_map.59 = (f32[120,512]{1,0:T(8,128)}, f32[1,120]{1,0:T(1,128)}) custom-call(s32[2,256]{1,0:T(2,128)} %pivots_ref.1, f32[480,384]{1,0:T(8,128)} %previous_ref.1, f32[120,512]{1,0:T(8,128)} %columns_ref.1, f32[1,120]{1,0:T(1,128)} %bitcast.2), custom_call_target="tpu_custom_call" | custom-call | tf_op jit(solution)/shard_map/pallas_call | solution.py:375
  90.6 0.0 copy-start
  90.6 1.7 %copy.8 = f32[120,512]{1,0:T(8,128)} copy(f32[120,512]{1,0:T(8,128)} %get-tuple-element.8) | data formatting | bytes 491520
  92.3 0.0 copy-done
  92.3 0.5 copy.9
Async XLA Ops:
  90.6 1.7 %copy-start = (f32[1,120]{1,0:T(1,128)S(1)}, f32[1,120]{1,0:T(1,128)}, u32[]{:S(2)}) copy-start(f32[1,120]{1,0:T(1,128)} %get-tuple-element.5) | copy-start | bytes 1444

commit v4 on v3

v4 whole, which is shorter than its diff:
```python
import functools

import jax
import jax.numpy as jnp
from jax import lax
from jax.experimental import pallas as pl
from jax.experimental.pallas import tpu as pltpu
from jax.sharding import PartitionSpec as P

HIGHEST = lax.Precision.HIGHEST
MESH = pl.DeviceIdType.MESH
BLOCK = 128
BLOCKS = 4
HALF = BLOCK // 2
EARLY = 384
SIDE = 8
REPS = 4
COUNTS = (BLOCK, (BLOCKS - 1) * BLOCK, (BLOCKS - 1) * BLOCK)
LANES = (EARLY + BLOCK, EARLY, BLOCK)
ORDER = (4, 3, 5, 2, 6, 1, 7)
BASE = 32
TILES = BASE // 8


def dot_tn(left, right):
    return lax.dot_general(
        left, right, (((0,), (0,)), ((), ())), precision=HIGHEST, preferred_element_type=jnp.float32
    )


def spread(tile, row):
    return jnp.broadcast_to(tile[row:row + 1, :], tile.shape)


def eliminate(square, wide):
    sub = lax.broadcasted_iota(jnp.int32, (8, 128), 0)
    cols = []
    for k in range(BASE):
        cols.append([None] * TILES)
        for v in range(k // 8, TILES):
            cols[k][v] = jnp.broadcast_to(square[8 * v:8 * v + 8, k:k + 1], (8, 128))
    lanes = wide.shape[1] // 128
    work = [[wide[8 * v:8 * v + 8, 128 * l:128 * l + 128] for l in range(lanes)] for v in range(TILES)]
    pivots = []
    for j in range(BASE):
        top, row = j // 8, j % 8
        pivot = spread(cols[j][top], row)
        pivots.append(pivot)
        inverse = 1.0 / pivot
        factor = [None] * TILES
        for v in range(top, TILES):
            value = cols[j][v] * inverse
            factor[v] = jnp.where(sub > row, value, 0.0) if v == top else value
        for k in range(j + 1, BASE):
            value = spread(cols[j][k // 8], k % 8)
            for v in range(k // 8, TILES):
                cols[k][v] = cols[k][v] - factor[v] * value
        for l in range(lanes):
            value = spread(work[top][l], row)
            for v in range(top, TILES):
                work[v][l] = work[v][l] - factor[v] * value
    out = []
    for v in range(TILES):
        pivot = pivots[8 * v]
        for s in range(1, 8):
            pivot = jnp.where(sub == s, pivots[8 * v + s], pivot)
        scale = lax.rsqrt(pivot)
        scale = scale * (1.5 - 0.5 * pivot * scale * scale)
        out.append(jnp.concatenate([work[v][l] * scale for l in range(lanes)], axis=1))
    return jnp.concatenate(out, axis=0)


def dot_nt(left, right, precision=HIGHEST):
    return lax.dot_general(
        left, right, (((1,), (1,)), ((), ())), precision=precision, preferred_element_type=jnp.float32
    )


def split(values):
    parts = []
    for _ in range(3):
        part = values.astype(jnp.bfloat16)
        values = values - part.astype(jnp.float32)
        parts.append(part)
    return parts


def pick(mask, parts):
    total = None
    for part in parts:
        term = lax.dot_general(mask, part, (((0,), (0,)), ((), ())), preferred_element_type=jnp.float32)
        total = term if total is None else total + term
    return total


def block_cols(s):
    return slice(s * BLOCK, s * BLOCK + BLOCK)


def kernel(pivots_ref, previous_ref, columns_ref, diagonal_ref, vectors_ref, diag_ref, *scratch):
    picks, pairs, halves, firsts, owns, seconds, fulls = (scratch[3 * n:3 * n + 3] for n in range(7))
    scratch = scratch[21:]
    gparts, gxs, gaccs, gsums = (scratch[BLOCKS * n:BLOCKS * n + BLOCKS] for n in range(4))
    scratch = scratch[4 * BLOCKS:]
    partials, rress, raccs = scratch[:2], scratch[2:4], scratch[4:6]
    prev_parts, slices, extra, upper, lower, inverse, parts = scratch[6:13]
    swap_sems, pair_sems, axis_sems, fwd_sems, gx_sems, gpair_sems, res_sems = scratch[13:]
    rows = lax.axis_index("rows")
    rep = lax.axis_index("rep")
    core = lax.rem(rows, 2)
    chip_z = lax.rem(rows // 2, SIDE)
    chip_y = rows // (2 * SIDE)
    spot = (1 - core) * chip_y + core * chip_z
    block_rows = previous_ref.shape[0]
    own_rows = columns_ref.shape[0]

    def at(y, z, c):
        return (y * SIDE + z) * 2 + c

    def first_peer(d):
        y = lax.rem(chip_y + (1 - core) * d, SIDE)
        z = lax.rem(chip_z + core * d, SIDE)
        return at(y, z, core), lax.rem(spot + d, SIDE)

    def second_peer(d):
        y = lax.rem(chip_y + core * d, SIDE)
        z = lax.rem(chip_z + (1 - core) * d, SIDE)
        return at(y, z, core)

    partner = at(chip_y, chip_z, 1 - core)
    turn = (1 - 2 * lax.rem(rep, 2)) * (1 - 2 * core)
    near = lax.rem(rep + turn + REPS, REPS)
    next_near = lax.rem(rep - turn + REPS, REPS)
    opposite = lax.rem(rep + 2, REPS)
    barrier = pltpu.get_barrier_semaphore()
    for d in range(1, SIDE):
        pl.semaphore_signal(barrier, inc=1, device_id=(first_peer(d)[0], rep), device_id_type=MESH)
        pl.semaphore_signal(barrier, inc=1, device_id=(second_peer(d), rep), device_id_type=MESH)
    for d in range(1, REPS):
        pl.semaphore_signal(barrier, inc=1, device_id=(rows, lax.rem(rep + d, REPS)), device_id_type=MESH)
    pl.semaphore_signal(barrier, inc=1, device_id=(partner, rep), device_id_type=MESH)

    def send(src, dst, sems, slot, where):
        copy = pltpu.make_async_remote_copy(
            src_ref=src, dst_ref=dst, send_sem=sems.at[(0,) + slot], recv_sem=sems.at[(1,) + slot],
            device_id=where, device_id_type=MESH,
        )
        copy.start()
        return copy

    flying = {}

    def index_of(s):
        return pivots_ref[s // 2:s // 2 + 1, block_cols(s % 2)]

    def block_mask(index):
        place = lax.broadcasted_iota(jnp.int32, (block_rows, index.shape[1]), 0) + rows * block_rows
        return jnp.where(place == index, 1.0, 0.0).astype(jnp.bfloat16)

    def pick_first():
        for n, part in enumerate(split(previous_ref[...])):
            prev_parts[n] = part
        picks[0][:, :EARLY] = pick(block_mask(index_of(0)), [prev_parts[n] for n in range(3)])
        place = lax.broadcasted_iota(jnp.int32, (BLOCK, BLOCK), 0)
        own = place + (rows * REPS + rep) * own_rows
        mask = jnp.where((own == index_of(0)) & (place < own_rows), 1.0, 0.0).astype(jnp.bfloat16)
        pad = jnp.zeros((BLOCK - own_rows, BLOCK), jnp.float32)
        found = pick(mask, split(jnp.concatenate([columns_ref[:, :BLOCK], pad], axis=0)))
        picks[0][:, EARLY:] = 0.5 * (found + found.T)

    def swap():
        flying["swap"] = []
        here = pl.ds(rep * own_rows, own_rows)
        for d in (2, 1, 3):
            other = lax.rem(rep + d, REPS)
            src = columns_ref.at[:, pl.ds(pl.multiple_of(other * BLOCK, BLOCK), BLOCK)]
            flying["swap"].append(send(src, slices.at[here, :], swap_sems, (d - 1,), (rows, other)))
        slices[here, :] = columns_ref[:, pl.ds(pl.multiple_of(rep * BLOCK, BLOCK), BLOCK)]
        extra[here, :] = columns_ref[:, block_cols(1)]
        for d in (2, 1, 3):
            other = lax.rem(rep + d, REPS)

            @pl.when(other == 2)
            def _():
                send(columns_ref.at[:, block_cols(1)], extra.at[here, :], swap_sems, (d + 2,), (rows, other)).wait_send()

    def pick_rest_early():
        index = jnp.concatenate([index_of(s) for s in range(1, BLOCKS)], axis=1)
        picks[1][...] = pick(block_mask(index), [prev_parts[n] for n in range(3)])

    def pick_rest_late():
        for copy in flying["swap"]:
            copy.wait()

        @pl.when(rep == 2)
        def _():
            here = pl.ds(rep * own_rows, own_rows)
            for d in (2, 1, 3):
                pltpu.make_async_remote_copy(
                    src_ref=columns_ref.at[:, block_cols(1)], dst_ref=extra.at[here, :], send_sem=swap_sems.at[0, d + 2],
                    recv_sem=swap_sems.at[1, d + 2], device_id=(rows, lax.rem(rep + d, REPS)), device_id_type=MESH,
                ).wait_recv()

        found = jnp.where(rep == 2, extra[...], slices[...])
        picks[2][:BLOCK, :] = pick(block_mask(jnp.where(rep == 2, index_of(0), index_of(1))), split(found))
        index = jnp.concatenate([index_of(s) for s in range(2, BLOCKS)], axis=1)
        picks[2][BLOCK:, :] = pick(block_mask(index), split(slices[...]))

    def pair(s):
        half, chunk = COUNTS[s] // 2, COUNTS[s] // 2 // SIDE
        src = picks[s].at[pl.ds((1 - core) * half, half), :]
        flying["pair", s] = send(src, pairs[s], pair_sems, (s,), (partner, rep))

    def first(s):
        half, chunk = COUNTS[s] // 2, COUNTS[s] // 2 // SIDE
        flying["pair", s].wait()
        halves[s][...] = picks[s][pl.ds(core * half, half), :] + pairs[s][...]
        flying["first", s] = []
        for d in ORDER:
            peer, place = first_peer(d)
            src = halves[s].at[pl.ds(place * chunk, chunk), :]
            flying["first", s].append(send(src, firsts[s].at[d - 1], axis_sems, (s, 0, d - 1), (peer, rep)))

    def second(s):
        half, chunk = COUNTS[s] // 2, COUNTS[s] // 2 // SIDE
        total = halves[s][pl.ds(spot * chunk, chunk), :]
        for copy in flying["first", s]:
            copy.wait()
        for d in range(1, SIDE):
            total = total + firsts[s][d - 1]
        owns[s][0] = total
        flying["second", s] = []
        for d in ORDER:
            where = (second_peer(d), rep)
            flying["second", s].append(send(owns[s].at[0], seconds[s].at[d - 1], axis_sems, (s, 1, d - 1), where))

    def gather(s):
        half, chunk = COUNTS[s] // 2, COUNTS[s] // 2 // SIDE
        for copy in flying["second", s]:
            copy.wait()
        total = owns[s][0]
        for d in range(1, SIDE):
            total = total + seconds[s][d - 1]
        owns[s][1] = total
        place = pl.ds(core * half + spot * chunk, chunk)
        fulls[s][place, :] = total
        flying["gather", s] = {}
        for d in ORDER:
            where = (first_peer(d)[0], rep)
            flying["gather", s][d] = send(owns[s].at[1], fulls[s].at[place, :], axis_sems, (s, 2, d - 1), where)
        flying["gather", s][0] = send(owns[s].at[1], fulls[s].at[place, :], fwd_sems, (s, 0), (partner, rep))

    def forward(s):
        half, chunk = COUNTS[s] // 2, COUNTS[s] // 2 // SIDE
        flying["forward", s] = []
        for d in (1, 7, 2, 6, 3, 5, 4):
            flying["gather", s][d].wait()
            source = lax.rem(spot + SIDE - d, SIDE)
            place = pl.ds(core * half + source * chunk, chunk)
            here = fulls[s].at[place, :]
            flying["forward", s].append(send(here, here, fwd_sems, (s, d), (partner, rep)))

    def landed(s):
        flying["gather", s][0].wait()
        for copy in flying["forward", s]:
            copy.wait()
        if s < 2:
            where = slice(0, BLOCK) if s == 0 else slice(BLOCK, BLOCKS * BLOCK)
            for n, part in enumerate(split(fulls[s][:, :EARLY])):
                parts[n, where, :] = part

    def products(left, left_rows, right_rows, terms):
        total = None
        for a, b in terms:
            term = lax.dot_general(
                left[a, left_rows, :], parts[b, right_rows, :], (((1,), (1,)), ((), ())),
                preferred_element_type=jnp.float32,
            )
            total = term if total is None else total + term
        return total

    def slot(s):
        return fulls[0][:, EARLY:] if s == 0 else fulls[2][(s - 1) * BLOCK:s * BLOCK, :]

    def weighed(place, value):
        return jnp.where(rep == place, value, 0.0)

    def column_part(s, t):
        value = slot(s)
        if s == 0:
            return value
        if t == s:
            return weighed(t, 0.5 * (value + value.T))
        if s == 1:
            return 0.5 * (weighed(0, value) + weighed(2, value.T))
        if (s, t) == (3, 2):
            return 0.5 * (weighed(2, value) + weighed(3, slot(2).T))
        return weighed(t, value)

    def gsum(s):
        terms = ((1, 1), (0, 2), (2, 0), (0, 1), (1, 0), (0, 0))
        gram = products(parts, block_cols(s), slice(0, s * BLOCK + BLOCK), terms)
        for t in range(s + 1):
            gparts[s][:, block_cols(t)] = column_part(s, t) - gram[:, block_cols(t)]
        mine = pl.ds(core * HALF, HALF)
        flying["gsum", s] = send(gparts[s].at[mine, :], gxs[s].at[0], gx_sems, (s, 0), (rows, near))

    def gnext(s):
        flying["gsum", s].wait()
        gaccs[s][...] = gparts[s][pl.ds(core * HALF, HALF), :] + gxs[s][0]
        flying["gnext", s] = send(gaccs[s].at[:, :], gxs[s].at[1], gx_sems, (s, 1), (rows, next_near))

    def gpair(s):
        mine = pl.ds(core * HALF, HALF)
        flying["gnext", s].wait()
        gsums[s][mine, :] = gaccs[s][...] + gxs[s][1]
        flying["gpair", s] = send(gsums[s].at[mine, :], gsums[s].at[mine, :], gpair_sems, (s,), (partner, rep))

    def rows_of(place):
        return pl.ds(place * own_rows, own_rows)

    def multiply(n):
        where = slice(0, BLOCK) if n == 0 else slice(BLOCK, BLOCKS * BLOCK)
        partials[n][...] = products(prev_parts, slice(None), where, ((0, 1), (1, 0), (0, 0)))

    def scatter(n):
        flying["scatter", n] = [
            send(partials[n].at[rows_of(place), :], rress[n].at[slot_of], res_sems, (n, slot_of), (rows, near))
            for slot_of, place in ((1, opposite), (0, near))
        ]

    def scatter_next(n):
        for copy in flying["scatter", n]:
            copy.wait()
        raccs[n][...] = partials[n][rows_of(next_near), :] + rress[n][1]
        flying["scatter_next", n] = send(raccs[n].at[:, :], rress[n].at[2], res_sems, (n, 2), (rows, next_near))

    def collect(n):
        flying["scatter_next", n].wait()
        total = (partials[n][rows_of(rep), :] + rress[n][0]) + rress[n][2]
        lanes = slice(0, BLOCK) if n == 0 else slice(BLOCK, BLOCKS * BLOCK)
        vectors_ref[:, lanes] = columns_ref[:, lanes] - total

    def update(s, t):
        done = dot_nt(vectors_ref[:, block_cols(t)], lower[s, :, block_cols(t)])
        vectors_ref[:, block_cols(s)] = vectors_ref[:, block_cols(s)] - done

    def solve(s):
        vectors_ref[:, block_cols(s)] = dot_nt(vectors_ref[:, block_cols(s)], inverse[s])

    def prepare(s, t):
        row = dot_nt(gsums[s][:, block_cols(t)], inverse[t])
        lower[s, :, block_cols(t)] = row
        for u in range(t + 1, s + 1):
            other = row if u == s else lower[u, :, block_cols(t)]
            gsums[s][:, block_cols(u)] = gsums[s][:, block_cols(u)] - dot_nt(row, other)

    def arrive(s):
        flying["gpair", s].wait()

    def factor(s, gaps):
        for k in range(BLOCK // BASE):
            here = slice(k * BASE, k * BASE + BASE)
            lane = lax.broadcasted_iota(jnp.int32, (BASE, BLOCK), 1)
            sub = lax.broadcasted_iota(jnp.int32, (BASE, BLOCK), 0)
            eye = jnp.where(lane == sub + k * BASE, 1.0, 0.0)
            wide = jnp.concatenate([gsums[s][here, block_cols(s)], eye], axis=1)
            for done in (slice(0, (k - 1) * BASE), slice(max(k - 1, 0) * BASE, k * BASE)):
                if done.stop > done.start:
                    wide = wide - dot_tn(upper[done, here], upper[done, :])
            for step in gaps.get(k, ()):
                step()
            upper[here, :] = eliminate(wide[:, here], wide)
        inverse[s] = upper[:, BLOCK:]

    def later(work, *which):
        return lambda: work(*which)

    pick_first()
    pick_rest_early()
    pl.semaphore_wait(barrier, 2 * (SIDE - 1) + REPS)
    pair(0)
    pair(1)
    swap()
    first(0)
    first(1)
    pick_rest_late()
    pair(2)
    second(0)
    first(2)
    second(1)
    gather(0)
    second(2)
    forward(0)
    landed(0)
    gsum(0)
    gather(1)
    gather(2)
    gnext(0)
    multiply(0)
    gpair(0)
    scatter(0)
    arrive(0)
    forward(1)
    forward(2)
    landed(1)
    landed(2)
    gsum(1)
    gsum(2)
    gsum(3)
    scatter_next(0)
    factor(0, {})
    gnext(1)
    gnext(2)
    gnext(3)
    gpair(1)
    multiply(1)
    scatter(1)
    collect(0)
    solve(0)
    arrive(1)
    prepare(1, 0)
    factor(1, {
        0: (later(gpair, 2),),
        1: (later(gpair, 3),),
        2: (later(arrive, 2), later(prepare, 2, 0)),
    })
    prepare(2, 1)
    factor(2, {
        0: (later(scatter_next, 1), later(arrive, 3), later(prepare, 3, 0)),
        1: (later(prepare, 3, 1),),
        3: (later(collect, 1), later(update, 1, 0)),
    })
    prepare(3, 2)
    factor(3, {
        0: (later(solve, 1), later(update, 2, 0)),
        1: (later(update, 2, 1), later(update, 3, 0)),
        2: (later(solve, 2), later(update, 3, 1)),
        3: (later(update, 3, 2),),
    })
    solve(3)
    ones = jnp.ones((8, BLOCK), jnp.float32)
    sums = diagonal_ref[...]
    for s in range(BLOCKS):
        vec = vectors_ref[:, block_cols(s)]
        sums = sums - dot_nt(ones, vec * vec)[0:1, :]
    diag_ref[...] = sums


def per_device(pivots, previous, columns, diagonal):
    f32 = jnp.float32
    own_rows = columns.shape[0]
    block_rows = previous.shape[0]
    vmem = lambda *shape: pltpu.VMEM(shape, f32)
    each = lambda build: [build(s) for s in range(BLOCKS)]
    scratch = []
    for build in (
        lambda n, w: vmem(n, w), lambda n, w: vmem(n // 2, w), lambda n, w: vmem(n // 2, w),
        lambda n, w: vmem(SIDE - 1, n // 2 // SIDE, w), lambda n, w: vmem(2, n // 2 // SIDE, w),
        lambda n, w: vmem(SIDE - 1, n // 2 // SIDE, w), lambda n, w: vmem(n, w),
    ):
        scratch += [build(n, w) for n, w in zip(COUNTS, LANES)]
    scratch += each(lambda s: vmem(BLOCK, BLOCK * (s + 1)))
    scratch += each(lambda s: vmem(2, HALF, BLOCK * (s + 1)))
    scratch += each(lambda s: vmem(HALF, BLOCK * (s + 1)))
    scratch += each(lambda s: vmem(BLOCK, BLOCK * (s + 1)))
    scratch += [vmem(block_rows, n) for n in COUNTS[:2]]
    scratch += [vmem(REPS - 1, own_rows, n) for n in COUNTS[:2]]
    scratch += [vmem(own_rows, n) for n in COUNTS[:2]]
    scratch += [
        pltpu.VMEM((3, block_rows, EARLY), jnp.bfloat16), vmem(block_rows, BLOCK), vmem(block_rows, BLOCK),
        vmem(BLOCK, 2 * BLOCK), vmem(BLOCKS, BLOCK, BLOCKS * BLOCK), vmem(BLOCKS, BLOCK, BLOCK),
        pltpu.VMEM((3, BLOCKS * BLOCK, EARLY), jnp.bfloat16),
    ]
    dma = pltpu.SemaphoreType.DMA
    scratch += [
        dma((2, 2 * (REPS - 1))), dma((2, 3)), dma((2, 3, 3, SIDE - 1)), dma((2, 3, SIDE)),
        dma((2, BLOCKS, 2)), dma((2, BLOCKS)), dma((2, 2, REPS - 1)),
    ]
    space = pl.BlockSpec(memory_space=pltpu.VMEM)
    vectors, diag = pl.pallas_call(
        kernel,
        out_shape=(jax.ShapeDtypeStruct(columns.shape, f32), jax.ShapeDtypeStruct((1, own_rows), f32)),
        in_specs=[space] * 4,
        out_specs=[space] * 2,
        scratch_shapes=scratch,
        compiler_params=pltpu.CompilerParams(collective_id=0, has_side_effects=True),
    )(pivots, previous, columns, diagonal.reshape(1, own_rows))
    return vectors, diag.reshape(own_rows)


def solution(mesh):
    placed = (P(), P("rows", "rep"), P(("rows", "rep"), None), P(("rows", "rep")))
    return jax.shard_map(
        per_device,
        mesh=mesh,
        in_specs=placed,
        out_specs=(P(("rows", "rep"), None), P(("rows", "rep"))),
        check_vma=False,
    )
```

time: 93 us -> 78.3 us (0.84); the launches traced: 92.8 us -> 77 us
  Pallas kernels: 90 us -> 74.1 us
    pallas_call x1, Pallas kernels: 90 us -> 74.1 us  [per_device(): pl.pallas_call(kernel, out_shape=(jax.ShapeDtypeStruct(columns.shape, f32...]
where the time goes in v4:
time: 78.3 us; the launch traced here: 77 us
  Pallas kernels  74.1 us (95%)
  local copies, waits for them, and re-layouts  2.17 us (3%)
    pallas_call x1, Pallas kernels, per_device(): pl.pallas_call(kernel, out_shape=(jax.ShapeDtypeStruct(columns.shape, f32...  74.1 us
    unnamed x4, local copies, waits for them, and re-layouts  2.17 us

profile of v4, /device:TPU:1, one launch (start us, length us, event | category | flops | bytes accessed | tf_op | source)
XLA Modules:
  0.0 77.0 jit_solution(8449226848830881165)
XLA Ops:
  0.6 74.1 %shard_map.59 = (f32[120,512]{1,0:T(8,128)}, f32[1,120]{1,0:T(1,128)}) custom-call(s32[2,256]{1,0:T(2,128)} %pivots_ref.1, f32[480,384]{1,0:T(8,128)} %previous_ref.1, f32[120,512]{1,0:T(8,128)} %columns_ref.1, f32[1,120]{1,0:T(1,128)} %bitcast.2), custom_call_target="tpu_custom_call" | custom-call | tf_op jit(solution)/shard_map/pallas_call | solution.py:481
  74.8 0.0 copy-start
  74.8 1.7 %copy.8 = f32[120,512]{1,0:T(8,128)} copy(f32[120,512]{1,0:T(8,128)} %get-tuple-element.8) | data formatting | bytes 491520
  76.5 0.0 copy-done
  76.5 0.5 copy.9
Async XLA Ops:
  74.8 1.7 %copy-start = (f32[1,120]{1,0:T(1,128)S(1)}, f32[1,120]{1,0:T(1,128)}, u32[]{:S(2)}) copy-start(f32[1,120]{1,0:T(1,128)} %get-tuple-element.5) | copy-start | bytes 1444

commit v5 on v4

--- a/solution.py
+++ b/solution.py
@@ -341,9 +341,10 @@
         lanes = slice(0, BLOCK) if n == 0 else slice(BLOCK, BLOCKS * BLOCK)
         vectors_ref[:, lanes] = columns_ref[:, lanes] - total
 
-    def update(s, t):
-        done = dot_nt(vectors_ref[:, block_cols(t)], lower[s, :, block_cols(t)])
-        vectors_ref[:, block_cols(s)] = vectors_ref[:, block_cols(s)] - done
+    def update(t):
+        below = lower[t + 1:, :, block_cols(t)].reshape((BLOCKS - 1 - t) * BLOCK, BLOCK)
+        lanes = slice((t + 1) * BLOCK, BLOCKS * BLOCK)
+        vectors_ref[:, lanes] = vectors_ref[:, lanes] - dot_nt(vectors_ref[:, block_cols(t)], below)
 
     def solve(s):
         vectors_ref[:, block_cols(s)] = dot_nt(vectors_ref[:, block_cols(s)], inverse[s])
@@ -351,9 +352,17 @@
     def prepare(s, t):
         row = dot_nt(gsums[s][:, block_cols(t)], inverse[t])
         lower[s, :, block_cols(t)] = row
-        for u in range(t + 1, s + 1):
-            other = row if u == s else lower[u, :, block_cols(t)]
-            gsums[s][:, block_cols(u)] = gsums[s][:, block_cols(u)] - dot_nt(row, other)
+        below = lower[t + 1:s + 1, :, block_cols(t)].reshape((s - t) * BLOCK, BLOCK)
+        lanes = slice((t + 1) * BLOCK, (s + 1) * BLOCK)
+        gsums[s][:, lanes] = gsums[s][:, lanes] - dot_nt(row, below)
+
+    def squares():
+        total = None
+        for s in range(BLOCKS):
+            vec = vectors_ref[:, block_cols(s)]
+            total = vec * vec if total is None else total + vec * vec
+        ones = jnp.ones((8, BLOCK), jnp.float32)
+        diag_ref[...] = diagonal_ref[...] - dot_nt(ones, total)[0:1, :]
 
     def arrive(s):
         flying["gpair", s].wait()
@@ -365,9 +374,9 @@
             sub = lax.broadcasted_iota(jnp.int32, (BASE, BLOCK), 0)
             eye = jnp.where(lane == sub + k * BASE, 1.0, 0.0)
             wide = jnp.concatenate([gsums[s][here, block_cols(s)], eye], axis=1)
-            for done in (slice(0, (k - 1) * BASE), slice(max(k - 1, 0) * BASE, k * BASE)):
-                if done.stop > done.start:
-                    wide = wide - dot_tn(upper[done, here], upper[done, :])
+            if k:
+                done = slice(0, k * BASE)
+                wide = wide - dot_tn(upper[done, here], upper[done, :])
             for step in gaps.get(k, ()):
                 step()
             upper[here, :] = eliminate(wide[:, here], wide)
@@ -429,22 +438,16 @@
     factor(2, {
         0: (later(scatter_next, 1), later(arrive, 3), later(prepare, 3, 0)),
         1: (later(prepare, 3, 1),),
-        3: (later(collect, 1), later(update, 1, 0)),
     })
     prepare(3, 2)
     factor(3, {
-        0: (later(solve, 1), later(update, 2, 0)),
-        1: (later(update, 2, 1), later(update, 3, 0)),
-        2: (later(solve, 2), later(update, 3, 1)),
-        3: (later(update, 3, 2),),
+        0: (later(collect, 1), later(update, 0)),
+        1: (later(solve, 1), later(update, 1)),
+        2: (later(solve, 2),),
+        3: (later(update, 2),),
     })
     solve(3)
-    ones = jnp.ones((8, BLOCK), jnp.float32)
-    sums = diagonal_ref[...]
-    for s in range(BLOCKS):
-        vec = vectors_ref[:, block_cols(s)]
-        sums = sums - dot_nt(ones, vec * vec)[0:1, :]
-    diag_ref[...] = sums
+    squares()
 
 
 def per_device(pivots, previous, columns, diagonal):

time: 78.3 us -> 76.9 us (0.982); the launches traced: 77 us -> 76.6 us
  no operation moved by 1% of the time
where the time goes in v5:
time: 76.9 us; the launch traced here: 76.6 us
  Pallas kernels  73.8 us (96%)
  local copies, waits for them, and re-layouts  2.17 us (3%)
    pallas_call x1, Pallas kernels, per_device(): pl.pallas_call(kernel, out_shape=(jax.ShapeDtypeStruct(columns.shape, f32...  73.8 us
    unnamed x4, local copies, waits for them, and re-layouts  2.17 us

profile of v5, /device:TPU:1, one launch (start us, length us, event | category | flops | bytes accessed | tf_op | source)
XLA Modules:
  0.0 76.6 jit_solution(6153858872769373137)
XLA Ops:
  0.6 73.8 %shard_map.59 = (f32[120,512]{1,0:T(8,128)}, f32[1,120]{1,0:T(1,128)}) custom-call(s32[2,256]{1,0:T(2,128)} %pivots_ref.1, f32[480,384]{1,0:T(8,128)} %previous_ref.1, f32[120,512]{1,0:T(8,128)} %columns_ref.1, f32[1,120]{1,0:T(1,128)} %bitcast.2), custom_call_target="tpu_custom_call" | custom-call | tf_op jit(solution)/shard_map/pallas_call | solution.py:484
  74.5 0.0 copy-start
  74.5 1.7 %copy.8 = f32[120,512]{1,0:T(8,128)} copy(f32[120,512]{1,0:T(8,128)} %get-tuple-element.8) | data formatting | bytes 491520
  76.1 0.0 copy-done
  76.1 0.5 copy.9
Async XLA Ops:
  74.5 1.7 %copy-start = (f32[1,120]{1,0:T(1,128)S(1)}, f32[1,120]{1,0:T(1,128)}, u32[]{:S(2)}) copy-start(f32[1,120]{1,0:T(1,128)} %get-tuple-element.5) | copy-start | bytes 1444

commit v6 on v5

--- a/solution.py
+++ b/solution.py
@@ -85,6 +85,12 @@
     return parts
 
 
+def dot_parts(left, right):
+    a, b = split(left), split(right)
+    terms = [dot_nt(a[m], b[n], None) for m, n in ((0, 1), (1, 0), (0, 0))]
+    return (terms[0] + terms[1]) + terms[2]
+
+
 def pick(mask, parts):
     total = None
     for part in parts:
@@ -344,10 +350,10 @@
     def update(t):
         below = lower[t + 1:, :, block_cols(t)].reshape((BLOCKS - 1 - t) * BLOCK, BLOCK)
         lanes = slice((t + 1) * BLOCK, BLOCKS * BLOCK)
-        vectors_ref[:, lanes] = vectors_ref[:, lanes] - dot_nt(vectors_ref[:, block_cols(t)], below)
+        vectors_ref[:, lanes] = vectors_ref[:, lanes] - dot_parts(vectors_ref[:, block_cols(t)], below)
 
     def solve(s):
-        vectors_ref[:, block_cols(s)] = dot_nt(vectors_ref[:, block_cols(s)], inverse[s])
+        vectors_ref[:, block_cols(s)] = dot_parts(vectors_ref[:, block_cols(s)], inverse[s])
 
     def prepare(s, t):
         row = dot_nt(gsums[s][:, block_cols(t)], inverse[t])
@@ -361,8 +367,9 @@
         for s in range(BLOCKS):
             vec = vectors_ref[:, block_cols(s)]
             total = vec * vec if total is None else total + vec * vec
-        ones = jnp.ones((8, BLOCK), jnp.float32)
-        diag_ref[...] = diagonal_ref[...] - dot_nt(ones, total)[0:1, :]
+        ones = jnp.ones((8, BLOCK), jnp.bfloat16)
+        sums = [dot_nt(ones, part, None) for part in split(total)]
+        diag_ref[...] = diagonal_ref[...] - ((sums[2] + sums[1]) + sums[0])[0:1, :]
 
     def arrive(s):
         flying["gpair", s].wait()

time: 76.9 us -> 76.8 us (level)
  no operation moved by 1% of the time
where the time goes in v6:
time: 76.8 us; the launch traced here: 76.5 us
  Pallas kernels  73.6 us (96%)
  local copies, waits for them, and re-layouts  2.17 us (3%)
    pallas_call x1, Pallas kernels, per_device(): pl.pallas_call(kernel, out_shape=(jax.ShapeDtypeStruct(columns.shape, f32...  73.6 us
    unnamed x4, local copies, waits for them, and re-layouts  2.17 us

profile of v6, /device:TPU:1, one launch (start us, length us, event | category | flops | bytes accessed | tf_op | source)
XLA Modules:
  0.0 76.5 jit_solution(10458352996417868867)
XLA Ops:
  0.6 73.6 %shard_map.59 = (f32[120,512]{1,0:T(8,128)}, f32[1,120]{1,0:T(1,128)}) custom-call(s32[2,256]{1,0:T(2,128)} %pivots_ref.1, f32[480,384]{1,0:T(8,128)} %previous_ref.1, f32[120,512]{1,0:T(8,128)} %columns_ref.1, f32[1,120]{1,0:T(1,128)} %bitcast.2), custom_call_target="tpu_custom_call" | custom-call | tf_op jit(solution)/shard_map/pallas_call | solution.py:491
  74.3 0.0 copy-start
  74.3 1.7 %copy.8 = f32[120,512]{1,0:T(8,128)} copy(f32[120,512]{1,0:T(8,128)} %get-tuple-element.8) | data formatting | bytes 491520
  75.9 0.0 copy-done
  75.9 0.5 copy.9
Async XLA Ops:
  74.3 1.7 %copy-start = (f32[1,120]{1,0:T(1,128)S(1)}, f32[1,120]{1,0:T(1,128)}, u32[]{:S(2)}) copy-start(f32[1,120]{1,0:T(1,128)} %get-tuple-element.5) | copy-start | bytes 1444
